TPU v7x, 256 devices: a whole 4x4x8 slice. The times are simulated.
256 devices in a mesh: dp: 8 (over x_hi, y), tensor: 32 (over z, x_lo, core).
Axes of the slice: x: 4 (x_hi: 2, x_lo: 2; x = x_hi * 2 + x_lo), y: 4, z: 8, core: 2. Of those that a mesh axis runs over, the one named last changes fastest.
Arguments:
- hidden: bfloat16 [4096, 16384], P('dp', 'tensor'), may hold values from -6 to 6
- down_weight: bfloat16 [16384, 8192], P('tensor'), may hold values from -0.046875 to 0.046875
- adapter_first_factor: bfloat16 [16384, 1024], P('tensor'), may hold values from -0.046875 to 0.046875
- adapter_second_factor: bfloat16 [1024, 8192], P(None, 'tensor'), may hold values from -1.5 to 1.5
- output_gradient: bfloat16 [4096, 8192], P(('dp', 'tensor')), may hold values from -6 to 6
- token_language_index: int32 [8, 512], P('dp'), may hold values from 0 to 63, never falling along the last dimension, each value on 1 to 128 neighbouring positions
- owned: int32 [64], replicated, may hold values from 0 to 63, each once
Outputs:
- mixed: bfloat16 [4096, 8192], P(('dp', 'tensor'))
- hidden_gradient: bfloat16 [4096, 16384], P('dp', 'tensor')
- grad_a: float32 [64, 16, 16384], P('dp', None, 'tensor')
- grad_b: float32 [64, 16, 8192], P('dp', None, 'tensor')
Inputs may be any that keep to these rules, and one draw needn't show every extreme that they name: Each row of token_language_index never falls and names every language; one language has exactly 128 tokens of the row, none more. `owned`: each adapter appears once.
All inputs are finite; a program needn't handle non-finite values.
Results may differ from a plain program's by a relative error of at most 0.0075.
Values may be sent and summed in bfloat16 or wider, within the bound.
A program may use at most 128 MiB of HBM per device.

v0:
```python
import jax
import jax.numpy as jnp
from jax import lax
from jax.sharding import PartitionSpec as P

ADAPTER_RANK = 16
LANGUAGE_COUNT = 64
adapter_scale = 0.5


def select_language_rank(full, language_mask):
    rows = full.shape[0]
    return jnp.sum(
        full.reshape(rows, LANGUAGE_COUNT, ADAPTER_RANK) * language_mask[:, :, None], axis=1
    )


def spread_rank(small, onehot_half):
    rows = small.shape[0]
    return (onehot_half[:, :, None] * small.astype(jnp.bfloat16)[:, None, :]).reshape(
        rows, LANGUAGE_COUNT * ADAPTER_RANK
    )


def contract_matrices(left, right, left_dim, right_dim):
    return lax.dot_general(
        left, right, (((left_dim,), (right_dim,)), ((), ())), preferred_element_type=jnp.float32
    )


def body(
    hidden,
    down_weight,
    adapter_first_factor,
    adapter_second_factor,
    output_gradient,
    token_language_index,
    owned,
):
    column_share = adapter_second_factor.shape[1]
    col_start = lax.axis_index("tensor") * column_share
    labels = token_language_index.reshape(-1)
    language_mask = (
        labels[:, None] == jnp.arange(LANGUAGE_COUNT, dtype=jnp.int32)[None, :]
    ).astype(jnp.float32)
    onehot_half = language_mask.astype(jnp.bfloat16)
    gathered = lax.all_gather(output_gradient, "tensor", axis=0, tiled=True)
    gradient_column_block = lax.dynamic_slice_in_dim(gathered, col_start, column_share, 1)
    frozen_input_gradient = contract_matrices(gathered, down_weight, 1, 1)
    rank_reduce_share = select_language_rank(
        jnp.dot(hidden, adapter_first_factor, preferred_element_type=jnp.float32), language_mask
    )
    input_gradient_share = select_language_rank(
        contract_matrices(gradient_column_block, adapter_second_factor, 1, 1), language_mask
    )
    rank_reduce, input_gradient = lax.psum((rank_reduce_share, input_gradient_share), "tensor")
    expanded_rank = spread_rank(rank_reduce, onehot_half)
    gradient_spread_rank = spread_rank(input_gradient, onehot_half)
    rank_expand = adapter_scale * jnp.dot(
        expanded_rank, adapter_second_factor, preferred_element_type=jnp.float32
    )
    base_rows = lax.psum_scatter(
        jnp.dot(hidden, down_weight, preferred_element_type=jnp.float32),
        "tensor",
        scatter_dimension=0,
        tiled=True,
    )
    lift_rows = lax.all_to_all(rank_expand, "tensor", split_axis=0, concat_axis=1, tiled=True)
    mixed = (base_rows + lift_rows).astype(jnp.bfloat16)
    hidden_gradient = (
        frozen_input_gradient
        + adapter_scale * contract_matrices(gradient_spread_rank, adapter_first_factor, 1, 1)
    ).astype(jnp.bfloat16)
    resident_first_factor = adapter_scale * contract_matrices(gradient_spread_rank, hidden, 0, 0)
    resident_second_factor = adapter_scale * contract_matrices(
        expanded_rank, gradient_column_block, 0, 0
    )
    ordered_a = jnp.take(
        resident_first_factor.reshape(LANGUAGE_COUNT, ADAPTER_RANK, -1), owned, axis=0
    )
    ordered_b = jnp.take(
        resident_second_factor.reshape(LANGUAGE_COUNT, ADAPTER_RANK, -1), owned, axis=0
    )
    grad_a, grad_b = (
        lax.psum_scatter(ordered_a, "dp", scatter_dimension=0, tiled=True),
        lax.psum_scatter(ordered_b, "dp", scatter_dimension=0, tiled=True),
    )
    return (mixed, hidden_gradient, grad_a, grad_b)


def solution(mesh):
    in_specs = (
        P("dp", "tensor"),
        P("tensor", None),
        P("tensor", None),
        P(None, "tensor"),
        P(("dp", "tensor"), None),
        P("dp", None),
        P(),
    )
    out_specs = (
        P(("dp", "tensor"), None),
        P("dp", "tensor"),
        P("dp", None, "tensor"),
        P("dp", None, "tensor"),
    )
    return jax.shard_map(body, mesh=mesh, in_specs=in_specs, out_specs=out_specs, check_vma=False)
```

profile of v0, /device:TPU:32, one launch (start us, length us, event | category | flops | bytes accessed | tf_op | source)
XLA Modules:
  0.0 457.7 jit_solution(10031234196702321765)
XLA Ops:
  7.2 0.0 copy-start
  7.2 0.0 all-gather.2.cloned.1.call-start
  7.2 0.7 all-gather.2.cloned.1.call-update
  7.9 0.0 reduce-scatter.4.cloned.1.call-start
  8.0 13.8 %fusion.9 = f32[512,8192]{1,0:T(8,128)} fusion(bf16[512,512]{1,0:T(8,128)(2,1)} %param.7, bf16[512,8192]{1,0:T(8,128)(2,1)} %param.8), kind=kOutput, calls=%fused_computation.26 | convolution fusion | flops 4294967296 | bytes 25690112 | tf_op jit(solution)/shard_map/dot_general | solution.py:63
  21.8 0.0 copy-start.10
  21.8 0.0 copy-start.9
  21.8 0.0 copy-start.1
  21.8 0.0 reduce-scatter.4.cloned.1.call-update
  21.8 0.0 copy-start.7
  21.8 0.0 reduce-scatter.8.cloned.1.call-start
  21.9 0.6 copy-done.10
  22.5 0.0 copy-done.9
  22.5 0.0 copy-done
  22.5 0.3 copy-done.1
  22.9 2.1 fusion.10
  25.0 59.6 %all-gather.2.cloned.1.call-done = bf16[512,8192]{1,0:T(8,128)(2,1)} async-done(((bf16[16,8192]{1,0:T(8,128)(2,1)}), bf16[512,8192]{1,0:T(8,128)(2,1)}) %all-gather.2.cloned.1.call-update) | async-done | bytes 8388624 | tf_op jit(solution)/shard_map/all_gather | solution.py:47
  84.6 0.0 copy-done.7
  84.6 0.0 copy-start.2
  84.6 1.6 fusion.3
  86.1 0.1 copy-done.2
  86.2 0.7 multiply_reduce_fusion
  86.9 102.4 %all-reduce = (bf16[512,16]{0,1:T(8,128)(2,1)S(1)}, bf16[512,16]{0,1:T(8,128)(2,1)S(1)}) all-reduce(f32[512,16]{0,1:T(8,128)S(1)} %get-tuple-element.5, f32[512,16]{0,1:T(8,128)S(1)} %get-tuple-element.4), channel_id=1, replica_groups=mesh['dp'=8,'tensor'=32] {'tensor'}, use_global_device_ids=true, to_apply=%region_2.0 | all-reduce | flops 16384 | bytes 98304 | tf_op jit(solution)/shard_map/psum | solution.py:56
  189.3 0.1 broadcast_multiply_fusion
  189.4 0.0 copy-start.5
  189.5 0.0 copy-start.3
  189.5 1.0 copy-done.5
  190.4 2.5 convolution_multiply_fusion.2
  192.9 2.9 gather_fusion.1
  195.8 2.4 broadcast_select_fusion.1
  198.2 0.0 reduce-scatter.8.cloned.1.call-update
  198.3 0.0 reduce-scatter.6.cloned.1.call-start
  198.3 0.0 copy-done.3
  198.3 2.1 convolution_multiply_fusion
  200.4 2.3 gather_fusion
  202.7 1.6 broadcast_select_fusion
  204.3 0.0 copy-start.6
  204.3 0.0 copy-start.8
  204.3 0.0 reduce-scatter.6.cloned.1.call-update
  204.3 1.2 copy-done.6
  205.5 0.1 copy-done.8
  205.6 1.3 convolution_multiply_fusion.3
  206.9 12.0 %all-to-all-start = ((f32[32,16,256]{2,1,0:T(8,128)}), f32[32,16,256]{2,1,0:T(8,128)S(1)}, u32[]{:S(2)}, u32[]{:S(2)}) async-start(f32[32,16,256]{2,1,0:T(8,128)} %bitcast.3), calls=%async_computation.1 | async-start | bytes 1048576 | tf_op jit(solution)/shard_map/all_to_all | solution.py:68
  218.9 0.0 copy-start.4
  218.9 9.7 %fusion.11 = f32[512,512]{1,0:T(8,128)S(1)} fusion(bf16[512,8192]{1,0:T(8,128)(2,1)} %all-gather.2.cloned.1.call-done, bf16[512,8192]{1,0:T(8,128)(2,1)} %param.8), kind=kOutput, calls=%fused_computation.28 | convolution fusion | flops 4294967296 | bytes 17825792 | tf_op jit(solution)/shard_map/dot_general | solution.py:26
  228.6 0.0 copy-done.4
  228.7 1.6 fusion.1
  230.2 8.5 %all-to-all-done = f32[32,16,256]{2,1,0:T(8,128)S(1)} async-done(((f32[32,16,256]{2,1,0:T(8,128)}), f32[32,16,256]{2,1,0:T(8,128)S(1)}, u32[]{:S(2)}, u32[]{:S(2)}) %all-to-all-start) | async-done | bytes 524320 | tf_op jit(solution)/shard_map/all_to_all | solution.py:68
  238.7 43.1 %reduce-scatter.4.cloned.1.call-done = f32[16,8192]{1,0:T(8,128)} async-done(((f32[512,8192]{1,0:T(8,128)}), f32[16,8192]{1,0:T(8,128)}) %reduce-scatter.4.cloned.1.call-update) | async-done | bytes 524304 | tf_op jit(solution)/shard_map/reduce_scatter | solution.py:62
  281.8 1.8 add_convert_fusion
  283.6 83.4 %reduce-scatter.8.cloned.1.call-done = f32[8,16,256]{2,1,0:T(8,128)} async-done(((f32[64,16,256]{2,1,0:T(8,128)}), f32[8,16,256]{2,1,0:T(8,128)}) %reduce-scatter.8.cloned.1.call-update) | async-done | bytes 131088 | tf_op jit(solution)/shard_map/reduce_scatter | solution.py:86
  367.0 84.2 %reduce-scatter.6.cloned.1.call-done = f32[8,16,512]{2,1,0:T(8,128)} async-done(((f32[64,16,512]{2,1,0:T(8,128)}), f32[8,16,512]{2,1,0:T(8,128)}) %reduce-scatter.6.cloned.1.call-update) | async-done | bytes 262160 | tf_op jit(solution)/shard_map/reduce_scatter | solution.py:85
  (5 shorter events, 0.1 us)
Async XLA Ops:
  7.2 15.4 %copy-start = (bf16[512,1024]{1,0:T(8,128)(2,1)S(1)}, bf16[512,1024]{1,0:T(8,128)(2,1)}, u32[]{:S(2)}) copy-start(bf16[512,1024]{1,0:T(8,128)(2,1)} %param.9) | copy-start | bytes 3145732
  7.2 77.4 %all-gather.2.cloned.1.call-start = ((), (), s32[]{:S(2)}) async-start(), calls=%async_computation.5 | async-start | bytes 8650752 | tf_op jit(solution)/shard_map/all_gather | solution.py:47
  7.9 273.9 %reduce-scatter.4.cloned.1.call-start = ((), (), s32[]{:S(2)}) async-start(), calls=%async_computation.4 | async-start | bytes 17301504 | tf_op jit(solution)/shard_map/reduce_scatter | solution.py:62
  21.8 0.7 copy-start.10
  21.8 0.7 copy-start.9
  21.8 1.1 copy-start.1
  21.8 62.7 %copy-start.7 = (bf16[1024,256]{1,0:T(8,128)(2,1)S(1)}, bf16[1024,256]{1,0:T(8,128)(2,1)}, u32[]{:S(2)}) copy-start(bf16[1024,256]{1,0:T(8,128)(2,1)} %param.10) | copy-start | bytes 1572868
  21.8 345.2 %reduce-scatter.8.cloned.1.call-start = ((), (), s32[]{:S(2)}) async-start(), calls=%async_computation.7 | async-start | bytes 1179648 | tf_op jit(solution)/shard_map/reduce_scatter | solution.py:86
  84.6 1.7 copy-start.2
  189.4 1.0 copy-start.5
  189.5 8.9 %copy-start.3 = (bf16[512,64,16]{0,2,1:T(8,128)(2,1)}, bf16[512,64,16]{0,2,1:T(8,128)(2,1)S(1)}, u32[]{:S(2)}) copy-start(bf16[512,64,16]{0,2,1:T(8,128)(2,1)S(1)} %get-tuple-element.8) | copy-start | bytes 3145732
  198.3 252.9 %reduce-scatter.6.cloned.1.call-start = ((), (), s32[]{:S(2)}) async-start(), calls=%async_computation.6 | async-start | bytes 2359296 | tf_op jit(solution)/shard_map/reduce_scatter | solution.py:85
  204.3 1.2 copy-start.6
  204.3 1.4 copy-start.8
  206.9 31.8 %all-to-all-start = ((f32[32,16,256]{2,1,0:T(8,128)}), f32[32,16,256]{2,1,0:T(8,128)S(1)}, u32[]{:S(2)}, u32[]{:S(2)}) async-start(f32[32,16,256]{2,1,0:T(8,128)} %bitcast.3), calls=%async_computation.1 | async-start | bytes 1048576 | tf_op jit(solution)/shard_map/all_to_all | solution.py:68
  218.9 9.8 %copy-start.4 = (bf16[512,64,16]{0,2,1:T(8,128)(2,1)S(1)}, bf16[512,64,16]{0,2,1:T(8,128)(2,1)}, u32[]{:S(2)}) copy-start(bf16[512,64,16]{0,2,1:T(8,128)(2,1)} %copy-done.3) | copy-start | bytes 3145732
Sparse Core Ops, SparseCore 0:
  9.9 74.6 all-gather.1
  87.1 194.6 reduce-scatter.3
  286.3 80.6 reduce-scatter.7
  372.0 79.1 reduce-scatter.5
where the time goes:
time: 458 us
  waiting for transfers between devices  279 us (61%)
  blocking collectives  102 us (22%)
  matrix products  34.6 us (8%)
  between operations  13.9 us (3%)
  starting transfers between devices  12.1 us (3%)
  local copies, waits for them, and re-layouts  8.59 us (2%)
  other arithmetic  6.66 us (1%)
    psum x1, blocking collectives, body(): lax.psum((rank_reduce_share, input_gradient_share), 'tensor')  102 us
    reduce_scatter x1, waiting for transfers between devices, body(): lax.psum_scatter(ordered_a, 'dp', scatter_dimension=0, tiled=True)  84.2 us
    reduce_scatter x1, waiting for transfers between devices, body(): lax.psum_scatter(ordered_b, 'dp', scatter_dimension=0, tiled=True)  83.4 us
    all_gather x1, waiting for transfers between devices, body(): gathered = lax.all_gather(output_gradient, 'tensor', axis=0, tiled=True)  59.6 us
    reduce_scatter x1, waiting for transfers between devices, body(): lax.psum_scatter(jnp.dot(hidden, down_weight, preferred_element_type=jnp....  43.1 us
    dot_general x5, matrix products, contract_matrices(): lax.dot_general(left, right, (((left_dim,), (right_dim,)), ((), ())), pre...  17.4 us
    dot_general x1, matrix products, body(): jnp.dot(hidden, down_weight, preferred_element_type=jnp.float32)  13.8 us
    all_to_all x1, starting transfers between devices, body(): lax.all_to_all(rank_expand, 'tensor', split_axis=0, concat_axis=1, tiled=...  12 us
  transfers between devices with their start and end apart: 5, of which 5 were waited for; matrix products, arithmetic and copies ran while one was open for 10% of the time, Pallas kernels for 0%

commit v1 on v0

--- a/solution.py
+++ b/solution.py
@@ -2,10 +2,16 @@
 import jax.numpy as jnp
 from jax import lax
 from jax.sharding import PartitionSpec as P
+from jax.lax import all_to_all, axis_size
 
 ADAPTER_RANK = 16
 LANGUAGE_COUNT = 64
 adapter_scale = 0.5
+
+
+def produce_matrix_over_axis(original):
+    current_arr = jnp.stack([original] * axis_size("tensor"))
+    return jnp.concatenate(all_to_all(current_arr, "tensor", 0, 0), axis=0)
 
 
 def select_language_rank(full, language_mask):
@@ -44,7 +50,7 @@
         labels[:, None] == jnp.arange(LANGUAGE_COUNT, dtype=jnp.int32)[None, :]
     ).astype(jnp.float32)
     onehot_half = language_mask.astype(jnp.bfloat16)
-    gathered = lax.all_gather(output_gradient, "tensor", axis=0, tiled=True)
+    gathered = produce_matrix_over_axis(output_gradient)
     gradient_column_block = lax.dynamic_slice_in_dim(gathered, col_start, column_share, 1)
     frozen_input_gradient = contract_matrices(gathered, down_weight, 1, 1)
     rank_reduce_share = select_language_rank(

time: 458 us -> 547 us (1.19)
  waiting for transfers between devices: 279 us -> 357 us
  starting transfers between devices: 12.1 us -> 21.1 us
    all_to_all x0 -> x1, waiting for transfers between devices: none -> 226 us  [produce_matrix_over_axis(): return jnp.concatenate(all_to_all(current_arr, 'tensor', 0, 0), axis=0)]
    all_gather x1 -> x0, waiting for transfers between devices: 59.6 us -> none  [body(): gathered = lax.all_gather(output_gradient, 'tensor', axis=0, tiled=True)]
    reduce_scatter x1, waiting for transfers between devices: 43.1 us -> 0.02 us  [body(): lax.psum_scatter(jnp.dot(hidden, down_weight, preferred_element_type=jnp....]
    reduce_scatter x1, waiting for transfers between devices: 83.4 us -> 40.8 us  [body(): lax.psum_scatter(ordered_b, 'dp', scatter_dimension=0, tiled=True)]
    all_to_all x0 -> x1, starting transfers between devices: none -> 9.84 us  [produce_matrix_over_axis(): return jnp.concatenate(all_to_all(current_arr, 'tensor', 0, 0), axis=0)]
  transfers between devices with their start and end apart: 5 -> 5, of which waited for: 5 -> 4; matrix products, arithmetic and copies ran while one was open for 10% -> 7% of each run, Pallas kernels for 0% -> 0%
where the time goes in v1:
time: 547 us
  waiting for transfers between devices  357 us (65%)
  blocking collectives  101 us (18%)
  matrix products  34.5 us (6%)
  starting transfers between devices  21.1 us (4%)
  between operations  13.9 us (3%)
  local copies, waits for them, and re-layouts  12.8 us (2%)
  other arithmetic  6.64 us (1%)
    all_to_all x1, waiting for transfers between devices, produce_matrix_over_axis(): return jnp.concatenate(all_to_all(current_arr, 'tensor', 0, 0), axis=0)  226 us
    psum x1, blocking collectives, body(): lax.psum((rank_reduce_share, input_gradient_share), 'tensor')  101 us
    reduce_scatter x1, waiting for transfers between devices, body(): lax.psum_scatter(ordered_a, 'dp', scatter_dimension=0, tiled=True)  84.2 us
    reduce_scatter x1, waiting for transfers between devices, body(): lax.psum_scatter(ordered_b, 'dp', scatter_dimension=0, tiled=True)  40.8 us
    dot_general x5, matrix products, contract_matrices(): lax.dot_general(left, right, (((left_dim,), (right_dim,)), ((), ())), pre...  17.3 us
    dot_general x1, matrix products, body(): jnp.dot(hidden, down_weight, preferred_element_type=jnp.float32)  13.9 us
    all_to_all x1, starting transfers between devices, body(): lax.all_to_all(rank_expand, 'tensor', split_axis=0, concat_axis=1, tiled=...  11.1 us
  transfers between devices with their start and end apart: 5, of which 4 were waited for; matrix products, arithmetic and copies ran while one was open for 7% of the time, Pallas kernels for 0%

profile of v1, /device:TPU:32, one launch (start us, length us, event | category | flops | bytes accessed | tf_op | source)
XLA Modules:
  0.0 546.7 jit_solution(292505652331290079)
XLA Ops:
  7.2 0.0 copy-start
  7.2 0.0 reduce-scatter.4.cloned.1.call-start
  7.2 13.9 %fusion.9 = f32[512,8192]{1,0:T(8,128)} fusion(bf16[512,512]{1,0:T(8,128)(2,1)} %param.7, bf16[512,8192]{1,0:T(8,128)(2,1)} %param.8), kind=kOutput, calls=%fused_computation.26 | convolution fusion | flops 4294967296 | bytes 25690112 | tf_op jit(solution)/shard_map/dot_general | solution.py:69
  21.1 0.0 copy-start.9
  21.1 0.0 reduce-scatter.4.cloned.1.call-update
  21.2 0.9 copy-done.9
  22.1 4.2 stack.2
  26.3 0.0 copy-start.11
  26.3 0.0 copy-start.10
  26.3 0.0 copy-start.1
  26.3 9.8 %all-to-all-start.1 = ((bf16[32,16,8192]{2,1,0:T(8,128)(2,1)}), bf16[32,16,8192]{2,1,0:T(8,128)(2,1)}, u32[]{:S(2)}, u32[]{:S(2)}) async-start(bf16[32,16,8192]{2,1,0:T(8,128)(2,1)} %stack.2), calls=%async_computation.2 | async-start | bytes 16777216 | tf_op jit(solution)/shard_map/all_to_all | solution.py:14
  36.2 0.0 copy-start.7
  36.2 0.0 reduce-scatter.8.cloned.1.call-start
  36.2 0.0 copy-done.11
  36.3 0.0 copy-done.10
  36.3 0.0 copy-done
  36.3 0.0 copy-done.1
  36.3 2.1 fusion.10
  38.4 225.8 %all-to-all-done.1 = bf16[32,16,8192]{2,1,0:T(8,128)(2,1)} async-done(((bf16[32,16,8192]{2,1,0:T(8,128)(2,1)}), bf16[32,16,8192]{2,1,0:T(8,128)(2,1)}, u32[]{:S(2)}, u32[]{:S(2)}) %all-to-all-start.1) | async-done | bytes 8388640 | tf_op jit(solution)/shard_map/all_to_all | solution.py:14
  264.2 0.0 copy-start.2
  264.2 0.0 copy-done.7
  264.2 1.6 fusion.3
  265.8 0.1 copy-done.2
  265.9 0.7 multiply_reduce_fusion
  266.6 101.2 %all-reduce = (bf16[512,16]{0,1:T(8,128)(2,1)S(1)}, bf16[512,16]{0,1:T(8,128)(2,1)S(1)}) all-reduce(f32[512,16]{0,1:T(8,128)S(1)} %get-tuple-element.5, f32[512,16]{0,1:T(8,128)S(1)} %get-tuple-element.4), channel_id=1, replica_groups=mesh['dp'=8,'tensor'=32] {'tensor'}, use_global_device_ids=true, to_apply=%region_2.0 | all-reduce | flops 16384 | bytes 98304 | tf_op jit(solution)/shard_map/psum | solution.py:62
  367.8 0.1 broadcast_multiply_fusion
  367.9 0.0 copy-start.5
  367.9 0.0 copy-start.3
  367.9 1.0 copy-done.5
  368.9 2.4 convolution_multiply_fusion.2
  371.4 2.9 gather_fusion.1
  374.3 2.4 broadcast_select_fusion.1
  376.7 0.0 reduce-scatter.8.cloned.1.call-update
  376.7 0.0 reduce-scatter.6.cloned.1.call-start
  376.7 0.0 copy-done.3
  376.8 2.1 convolution_multiply_fusion
  378.8 2.3 gather_fusion
  381.1 1.6 broadcast_select_fusion
  382.7 0.0 copy-start.6
  382.7 0.0 copy-start.8
  382.7 0.0 reduce-scatter.6.cloned.1.call-update
  382.7 1.2 copy-done.6
  383.9 0.1 copy-done.8
  384.1 1.3 convolution_multiply_fusion.3
  385.3 11.1 %all-to-all-start = ((f32[32,16,256]{2,1,0:T(8,128)}), f32[32,16,256]{2,1,0:T(8,128)S(1)}, u32[]{:S(2)}, u32[]{:S(2)}) async-start(f32[32,16,256]{2,1,0:T(8,128)} %bitcast.3), calls=%async_computation.1 | async-start | bytes 1048576 | tf_op jit(solution)/shard_map/all_to_all | solution.py:74
  396.4 0.0 copy-start.4
  396.5 9.6 %fusion.11 = f32[512,512]{1,0:T(8,128)S(1)} fusion(bf16[512,8192]{1,0:T(8,128)(2,1)} %bitcast.5, bf16[512,8192]{1,0:T(8,128)(2,1)} %param.8), kind=kOutput, calls=%fused_computation.28 | convolution fusion | flops 4294967296 | bytes 17825792 | tf_op jit(solution)/shard_map/dot_general | solution.py:32
  406.1 0.0 copy-done.4
  406.1 1.6 fusion.1
  407.6 5.6 %all-to-all-done = f32[32,16,256]{2,1,0:T(8,128)S(1)} async-done(((f32[32,16,256]{2,1,0:T(8,128)}), f32[32,16,256]{2,1,0:T(8,128)S(1)}, u32[]{:S(2)}, u32[]{:S(2)}) %all-to-all-start) | async-done | bytes 524320 | tf_op jit(solution)/shard_map/all_to_all | solution.py:74
  413.3 0.0 reduce-scatter.4.cloned.1.call-done
  413.3 1.8 add_convert_fusion
  415.1 40.8 %reduce-scatter.8.cloned.1.call-done = f32[8,16,256]{2,1,0:T(8,128)} async-done(((f32[64,16,256]{2,1,0:T(8,128)}), f32[8,16,256]{2,1,0:T(8,128)}) %reduce-scatter.8.cloned.1.call-update) | async-done | bytes 131088 | tf_op jit(solution)/shard_map/reduce_scatter | solution.py:92
  456.0 84.2 %reduce-scatter.6.cloned.1.call-done = f32[8,16,512]{2,1,0:T(8,128)} async-done(((f32[64,16,512]{2,1,0:T(8,128)}), f32[8,16,512]{2,1,0:T(8,128)}) %reduce-scatter.6.cloned.1.call-update) | async-done | bytes 262160 | tf_op jit(solution)/shard_map/reduce_scatter | solution.py:91
  (5 shorter events, 0.1 us)
Async XLA Ops:
  7.2 29.2 %copy-start = (bf16[512,1024]{1,0:T(8,128)(2,1)S(1)}, bf16[512,1024]{1,0:T(8,128)(2,1)}, u32[]{:S(2)}) copy-start(bf16[512,1024]{1,0:T(8,128)(2,1)} %param.9) | copy-start | bytes 3145732
  7.2 406.1 %reduce-scatter.4.cloned.1.call-start = ((), (), s32[]{:S(2)}) async-start(), calls=%async_computation.5 | async-start | bytes 17301504 | tf_op jit(solution)/shard_map/reduce_scatter | solution.py:68
  21.1 0.9 copy-start.9
  26.3 9.9 %copy-start.11 = (s32[64]{0:T(128)S(1)}, s32[64]{0:T(128)}, u32[]{:S(2)}) copy-start(s32[64]{0:T(128)} %param.13) | copy-start | bytes 772
  26.3 10.0 %copy-start.10 = (s32[1,512]{1,0:T(1,128)S(1)}, s32[1,512]{1,0:T(1,128)}, u32[]{:S(2)}) copy-start(s32[1,512]{1,0:T(1,128)} %param.12) | copy-start | bytes 6148
  26.3 10.0 %copy-start.1 = (bf16[512,512]{1,0:T(8,128)(2,1)S(1)}, bf16[512,512]{1,0:T(8,128)(2,1)}, u32[]{:S(2)}) copy-start(bf16[512,512]{1,0:T(8,128)(2,1)} %param.7) | copy-start | bytes 1572868
  26.3 237.9 %all-to-all-start.1 = ((bf16[32,16,8192]{2,1,0:T(8,128)(2,1)}), bf16[32,16,8192]{2,1,0:T(8,128)(2,1)}, u32[]{:S(2)}, u32[]{:S(2)}) async-start(bf16[32,16,8192]{2,1,0:T(8,128)(2,1)} %stack.2), calls=%async_computation.2 | async-start | bytes 16777216 | tf_op jit(solution)/shard_map/all_to_all | solution.py:14
  36.2 228.1 %copy-start.7 = (bf16[1024,256]{1,0:T(8,128)(2,1)S(1)}, bf16[1024,256]{1,0:T(8,128)(2,1)}, u32[]{:S(2)}) copy-start(bf16[1024,256]{1,0:T(8,128)(2,1)} %param.10) | copy-start | bytes 1572868
  36.2 419.8 %reduce-scatter.8.cloned.1.call-start = ((), (), s32[]{:S(2)}) async-start(), calls=%async_computation.7 | async-start | bytes 1179648 | tf_op jit(solution)/shard_map/reduce_scatter | solution.py:92
  264.2 1.7 copy-start.2
  367.9 1.0 copy-start.5
  367.9 8.8 %copy-start.3 = (bf16[512,64,16]{0,2,1:T(8,128)(2,1)}, bf16[512,64,16]{0,2,1:T(8,128)(2,1)S(1)}, u32[]{:S(2)}) copy-start(bf16[512,64,16]{0,2,1:T(8,128)(2,1)S(1)} %get-tuple-element.8) | copy-start | bytes 3145732
  376.7 163.5 %reduce-scatter.6.cloned.1.call-start = ((), (), s32[]{:S(2)}) async-start(), calls=%async_computation.6 | async-start | bytes 2359296 | tf_op jit(solution)/shard_map/reduce_scatter | solution.py:91
  382.7 1.2 copy-start.6
  382.7 1.4 copy-start.8
  385.3 27.9 %all-to-all-start = ((f32[32,16,256]{2,1,0:T(8,128)}), f32[32,16,256]{2,1,0:T(8,128)S(1)}, u32[]{:S(2)}, u32[]{:S(2)}) async-start(f32[32,16,256]{2,1,0:T(8,128)} %bitcast.3), calls=%async_computation.1 | async-start | bytes 1048576 | tf_op jit(solution)/shard_map/all_to_all | solution.py:74
  396.4 9.6 %copy-start.4 = (bf16[512,64,16]{0,2,1:T(8,128)(2,1)S(1)}, bf16[512,64,16]{0,2,1:T(8,128)(2,1)}, u32[]{:S(2)}) copy-start(bf16[512,64,16]{0,2,1:T(8,128)(2,1)} %copy-done.3) | copy-start | bytes 3145732
Sparse Core Ops, SparseCore 0:
  21.3 325.2 reduce-scatter.3
  376.8 79.0 reduce-scatter.7
  461.1 79.0 reduce-scatter.5
